TPU v7x, 32 devices: a whole 2x2x4 slice. The times are simulated.
32 devices in a mesh: group: 2 (over y), tensor: 4 (over z), dp: 4 (over x, core).
Axes of the slice: x: 2, y: 2, z: 4, core: 2. Of those that a mesh axis runs over, the one named last changes fastest.
Arguments:
- teacher_input: bfloat16 [16, 257, 6144], P(('group', 'dp')), parts along dimension 0, may hold values from -1000 to 1000
- teacher_gain: float32 [6144], replicated, may hold values from 0.5 to 2
- teacher_weight: bfloat16 [6144, 2, 6144], P('dp', None, 'tensor'), may hold values from -30 to 30
- head_counts: int32 [48, 16], replicated, may hold values from 0 to 3
- assignment: int32 [16], P(('group', 'dp')), parts along dimension 0, may hold values from 0 to 7, each once
- student_input: bfloat16 [16, 257, 1024], P(('group', 'dp')), parts along dimension 0, may hold values from -1000 to 1000
- student_gain: float32 [1024], replicated, may hold values from 0.5 to 2
- student_bias: float32 [1024], replicated, may hold values from -3 to 3
- student_weight: bfloat16 [1024, 2048], P(None, 'tensor'), may hold values from -30 to 30
Outputs:
- weight_grad: float32 [2048, 2048], P('group', 'tensor'), parts along dimension 0
There are 2 independent parts, one for each index of `group`. A program takes and returns all parts, laid end to end along the dimension named above; an argument that names none is the same for every part. Nothing has to cross between parts.
Inputs may be any that keep to these rules, and one draw needn't show every extreme that they name: `assignment`: every image index of the group appears exactly once.
All inputs are finite; a program needn't handle non-finite values.
Results may differ from a plain program's by a relative error of at most 0.013.
The roundings to bfloat16 on the way count: a program that leaves them out, or rounds other values in their place, can miss the bound.
Values may be sent and summed in bfloat16 or wider, within the bound.
A program may use at most 192 MiB of HBM per device.

v0:
```python
import jax
import jax.numpy as jnp
from jax import lax
from jax.sharding import PartitionSpec as P

HD_T = 128
D_S = 1024
HD_S = 64
QROWS = 128
DIVISOR = 72


def layer_norm(values, gain, shift):
    wide = values.astype(jnp.float32)
    center = wide - jnp.mean(wide, axis=-1, keepdims=True)
    spread = jnp.mean(center * center, axis=-1, keepdims=True)
    return center * lax.rsqrt(spread + 1e-06) * gain + shift


def on_device(
    teacher_input,
    teacher_gain,
    teacher_weight,
    head_counts,
    assignment,
    student_input,
    student_gain,
    student_bias,
    student_weight,
):
    images = teacher_input.shape[0]
    tokens = teacher_input.shape[1]
    width_t = teacher_input.shape[2]
    teacher_cols = teacher_weight.shape[2]
    heads_here = teacher_cols // HD_T
    student_heads = student_weight.shape[1] // (2 * HD_S)
    tensor_place = lax.axis_index("tensor")
    teacher_normed = layer_norm(teacher_input, teacher_gain, 0.0).astype(jnp.bfloat16)
    normed_query = teacher_normed[:, :QROWS].reshape(images * QROWS, width_t)
    normed_keys = teacher_normed.reshape(images * tokens, width_t)
    piece = lax.all_gather(teacher_weight, "dp", axis=0, tiled=True)
    new_query = jnp.dot(normed_query, piece[:, 0, :], preferred_element_type=jnp.float32)
    new_keys = jnp.dot(normed_keys, piece[:, 1, :], preferred_element_type=jnp.float32)
    teacher_query = (
        (new_query * HD_T ** (-0.5)).astype(jnp.bfloat16).reshape(images, QROWS, heads_here, HD_T)
    )
    teacher_keys = new_keys.astype(jnp.bfloat16).reshape(images, tokens, heads_here, HD_T)
    teacher_scores = jnp.einsum(
        "bqhd,bkhd->bhqk", teacher_query, teacher_keys, preferred_element_type=jnp.float32
    )
    teacher_maps = jax.nn.softmax(teacher_scores, axis=-1).astype(jnp.bfloat16)
    own_counts = lax.dynamic_slice_in_dim(
        head_counts, tensor_place * heads_here, heads_here, 0
    ).astype(jnp.bfloat16)
    folded = lax.psum_scatter(
        (
            jnp.einsum(
                "bgqk,gs->sbqk", teacher_maps, own_counts, preferred_element_type=jnp.float32
            )
            / DIVISOR
        ).astype(jnp.bfloat16),
        "tensor",
        scatter_dimension=0,
        tiled=True,
    )
    piece = lax.all_gather(folded, "dp", axis=1, tiled=True)
    width_piece = piece.shape[1]
    positions = jnp.arange(width_piece, dtype=jnp.int32)
    picker = (assignment[:, None] == positions[None, :]).astype(jnp.bfloat16)
    target = jnp.einsum("ji,hiqk->hjqk", picker, piece, preferred_element_type=jnp.float32).astype(
        jnp.bfloat16
    )
    student_normed = layer_norm(student_input, student_gain, student_bias).astype(jnp.bfloat16)
    normed_front = student_normed[:, :QROWS]
    packed = student_weight.reshape(D_S, student_heads, 2, HD_S)
    weight_query = packed[:, :, 0, :].reshape(D_S, student_heads * HD_S)
    weight_key = packed[:, :, 1, :].reshape(D_S, student_heads * HD_S)
    student_query = (
        jnp.einsum("btd,dc->btc", normed_front, weight_query, preferred_element_type=jnp.float32)
        * HD_S ** (-0.5)
    ).astype(jnp.bfloat16)
    student_keys = jnp.einsum(
        "btd,dc->btc", student_normed, weight_key, preferred_element_type=jnp.float32
    ).astype(jnp.bfloat16)
    split_query = student_query.reshape(images, QROWS, student_heads, HD_S)
    split_keys = student_keys.reshape(images, tokens, student_heads, HD_S)
    probs = jax.nn.softmax(
        jnp.einsum("bqhd,bkhd->hbqk", split_query, split_keys, preferred_element_type=jnp.float32),
        axis=-1,
    )
    target_wide = target.astype(jnp.float32)
    score_grad = (probs * jnp.sum(target_wide, axis=-1, keepdims=True) - target_wide).astype(
        jnp.bfloat16
    )
    query_grad = (
        jnp.einsum("hbqk,bkhd->bqhd", score_grad, split_keys, preferred_element_type=jnp.float32)
        * HD_S ** (-0.5)
    ).astype(jnp.bfloat16)
    key_grad = jnp.einsum(
        "hbqk,bqhd->bkhd", score_grad, split_query, preferred_element_type=jnp.float32
    ).astype(jnp.bfloat16)
    grad_query = jnp.einsum(
        "fkm,fkp->mp",
        normed_front,
        query_grad.reshape(images, QROWS, student_heads * HD_S),
        preferred_element_type=jnp.float32,
    )
    grad_key = jnp.einsum(
        "oip,ois->ps",
        student_normed,
        key_grad.reshape(images, tokens, student_heads * HD_S),
        preferred_element_type=jnp.float32,
    )
    local_grad = jnp.stack(
        [grad_query.reshape(D_S, student_heads, HD_S), grad_key.reshape(D_S, student_heads, HD_S)],
        axis=2,
    )
    local_grad = local_grad.reshape(D_S, student_heads * 2 * HD_S)
    return lax.psum(local_grad.astype(jnp.bfloat16), "dp").astype(jnp.float32)


def solution(mesh):
    placed = (
        P(("group", "dp"), None, None),
        P(),
        P("dp", None, "tensor"),
        P(),
        P(("group", "dp")),
        P(("group", "dp"), None, None),
        P(),
        P(),
        P(None, "tensor"),
    )
    return jax.shard_map(
        on_device, mesh=mesh, in_specs=placed, out_specs=P("group", "tensor"), check_vma=False
    )
```

profile of v0, /device:TPU:0, one launch (start us, length us, event | category | flops | bytes accessed | tf_op | source)
XLA Modules:
  0.0 448.8 jit_solution(8952922629155033750)
XLA Ops:
  6.5 8.8 %copy.104 = bf16[1536,2,1536]{2,0,1:T(8,128)(2,1)} copy(bf16[1536,2,1536]{2,1,0:T(2,128)(2,1)} %param.11) | data formatting | bytes 18874368 | tf_op args[2]
  15.3 0.0 all-gather.3.cloned.1.call-update
  15.3 0.0 all-reduce.6.cloned.1.call-start
  15.4 6.3 %convert_reduce_fusion = f32[2,257]{1,0:T(2,128)S(1)} fusion(bf16[2,257,6144]{2,0,1:T(2,128)(2,1)} %param.9), kind=kLoop, calls=%fused_computation.6 | loop fusion | flops 6315518 | bytes 6318088 | tf_op jit(solution)/shard_map/reduce_sum | solution.py:15
  21.7 3.5 fusion.5
  25.2 4.1 fusion.7
  29.4 4.6 %copy-done.1 = bf16[2,257,6144]{2,1,0:T(8,128)(2,1)} copy-done((bf16[2,257,6144]{2,1,0:T(8,128)(2,1)}, bf16[2,257,6144]{2,1,0:T(8,128)(2,1)S(1)}, u32[]{:S(2)}) %copy-start.1) | copy-done | bytes 6316056
  34.0 9.8 %reshape.81 = bf16[514,6144]{1,0:T(8,128)(2,1)} reshape(bf16[2,257,6144]{2,1,0:T(8,128)(2,1)} %copy-done.1) | data formatting | bytes 12632064 | tf_op jit(solution)/shard_map/reshape | solution.py:40
  43.7 202.4 %all-gather.3.cloned.1.call-done = bf16[6144,2,1536]{2,0,1:T(8,128)(2,1)} async-done(((bf16[1536,2,1536]{2,0,1:T(8,128)(2,1)}), bf16[6144,2,1536]{2,0,1:T(8,128)(2,1)}) %all-gather.3.cloned.1.call-update) | async-done | bytes 37748752 | tf_op jit(solution)/shard_map/all_gather | solution.py:41
  246.1 10.2 %fusion.10 = bf16[256,1536]{1,0:T(8,128)(2,1)} fusion(bf16[256,6144]{1,0:T(8,128)(2,1)S(1)} %bitcast.99, bf16[6144,2,1536]{2,0,1:T(8,128)(2,1)} %all-gather.3.cloned.1.call-done), kind=kOutput, calls=%fused_computation.19 | convolution fusion | flops 4832624640 | bytes 22806528 | tf_op jit(solution)/shard_map/dot_general | solution.py:42
  256.3 2.4 reshape.95
  258.6 16.2 %fusion.8 = bf16[514,1536]{1,0:T(8,128)(2,1)S(1)} fusion(bf16[514,6144]{1,0:T(8,128)(2,1)} %reshape.81, bf16[6144,2,1536]{2,0,1:T(8,128)(2,1)} %all-gather.3.cloned.1.call-done), kind=kOutput, calls=%fused_computation.15 | convolution fusion | flops 9702214656 | bytes 26843136 | tf_op jit(solution)/shard_map/dot_general | solution.py:43
  274.8 2.4 reshape.82
  277.2 3.1 fusion.61
  280.4 0.3 divide_convert_fusion
  280.6 0.4 copy-done.6
  281.1 0.8 multiply_convert_fusion
  281.8 2.9 copy.109
  284.8 0.0 all-reduce.6.cloned.1.call-update
  284.8 0.0 all-gather.5.cloned.1.call-start
  284.9 0.6 dynamic-slice
  286.1 85.7 %all-reduce.6.cloned.1.call-done = bf16[16,2,128,257]{2,1,3,0:T(2,128)(2,1)} async-done(((bf16[16,2,128,257]{2,1,3,0:T(2,128)(2,1)}), bf16[16,2,128,257]{2,1,3,0:T(2,128)(2,1)}) %all-reduce.6.cloned.1.call-update) | async-done | bytes 2105360
  371.8 1.4 constant_dynamic-slice_fusion
  373.2 1.0 copy.110
  374.3 0.0 all-reduce.4.cloned.1.call-start
  374.3 0.8 copy.94
  375.2 0.3 convert_reduce_fusion.1
  375.5 0.5 fusion.13
  376.0 0.1 fusion.60
  376.1 0.8 convolution_convert_fusion.1
  376.9 0.2 copy.96
  377.1 0.5 fusion.16
  377.6 1.0 copy-done.3
  378.6 0.3 fusion.27
  378.9 0.1 copy.98
  379.0 0.5 fusion.66
  379.6 0.5 fusion.34
  380.1 16.0 %all-gather.5.cloned.1.call-done = bf16[4,8,128,257]{2,0,3,1:T(4,128)(2,1)} async-done(((bf16[4,2,128,257]{2,0,3,1:T(4,128)(2,1)}), bf16[4,8,128,257]{2,0,3,1:T(4,128)(2,1)}) %all-gather.5.cloned.1.call-update) | async-done | bytes 2105360 | tf_op jit(solution)/shard_map/all_gather | solution.py:66
  396.1 2.4 fusion.17
  398.4 0.3 bitcast_reduce_fusion
  398.8 0.7 fusion.31
  399.4 1.5 fusion.24
  401.0 1.0 fusion.25
  402.0 0.1 pad_maximum_fusion
  402.1 1.1 copy.117
  403.2 0.0 all-reduce.4.cloned.1.call-update
  403.2 36.5 %all-reduce.4.cloned.1.call-done = bf16[1024,512]{0,1:T(8,128)(2,1)} async-done(((bf16[1024,512]{0,1:T(8,128)(2,1)}), bf16[1024,512]{0,1:T(8,128)(2,1)}) %all-reduce.4.cloned.1.call-update) | async-done | bytes 1048592 | tf_op jit(solution)/shard_map/psum | solution.py:119
  439.7 2.6 copy.118
  (28 shorter events, 0.1 us)
Async XLA Ops:
  6.5 239.5 %all-gather.3.cloned.1.call-start = ((), (), s32[]{:S(2)}) async-start(), calls=%async_computation | async-start | bytes 47185920 | tf_op jit(solution)/shard_map/all_gather | solution.py:41
  15.3 356.5 %all-reduce.6.cloned.1.call-start = ((), (), s32[]{:S(2)}) async-start(), calls=%async_computation.3 | async-start | bytes 4210688
  15.4 6.3 %copy-start = (bf16[2,257,6144]{2,0,1:T(2,128)(2,1)S(1)}, bf16[2,257,6144]{2,0,1:T(2,128)(2,1)}, u32[]{:S(2)}) copy-start(bf16[2,257,6144]{2,0,1:T(2,128)(2,1)} %param.9) | copy-start | bytes 18948100
  21.7 3.5 copy-start.5
  29.4 4.6 %copy-start.1 = (bf16[2,257,6144]{2,1,0:T(8,128)(2,1)}, bf16[2,257,6144]{2,1,0:T(8,128)(2,1)S(1)}, u32[]{:S(2)}) copy-start(bf16[2,257,6144]{2,1,0:T(8,128)(2,1)S(1)} %fusion.7) | copy-start | bytes 18948100
  34.0 212.1 %slice-start = ((bf16[2,257,6144]{2,1,0:T(8,128)(2,1)}), bf16[2,128,6144]{2,1,0:T(8,128)(2,1)S(1)}, s32[]{:S(2)}) async-start(bf16[2,257,6144]{2,1,0:T(8,128)(2,1)} %copy-done.1), calls=%async_computation.4 | async-start | bytes 6291456 | tf_op jit(solution)/shard_map/slice | solution.py:39
  280.4 0.7 copy-start.6
  281.8 3.0 copy-start.10
  284.8 89.5 %copy-start.4 = (bf16[1024,512]{1,0:T(8,128)(2,1)S(1)}, bf16[1024,512]{1,0:T(8,128)(2,1)}, u32[]{:S(2)}) copy-start(bf16[1024,512]{1,0:T(8,128)(2,1)} %param.17) | copy-start | bytes 3145732
  284.8 111.3 %all-gather.5.cloned.1.call-start = ((), (), s32[]{:S(2)}) async-start(), calls=%async_computation.1 | async-start | bytes 2631680 | tf_op jit(solution)/shard_map/all_gather | solution.py:66
  286.1 89.0 %copy-start.2 = (bf16[2,257,1024]{2,0,1:T(2,128)(2,1)S(1)}, bf16[2,257,1024]{2,0,1:T(2,128)(2,1)}, u32[]{:S(2)}) copy-start(bf16[2,257,1024]{2,0,1:T(2,128)(2,1)} %param.14) | copy-start | bytes 3158020
  374.3 65.4 %all-reduce.4.cloned.1.call-start = ((), (), s32[]{:S(2)}) async-start(), calls=%async_computation.2 | async-start | bytes 2097152 | tf_op jit(solution)/shard_map/psum | solution.py:119
  375.1 0.9 copy-start.7
  375.1 0.9 copy-start.8
  377.6 1.0 copy-start.3
  378.6 17.5 %copy-start.9 = (s32[2]{0:T(128)S(1)}, s32[2]{0:T(128)}, u32[]{:S(2)}) copy-start(s32[2]{0:T(128)} %param.13) | copy-start | bytes 28
Sparse Core Ops, SparseCore 0:
  15.5 230.5 all-gather.2
  284.9 86.8 all-reduce.5
  374.4 21.6 all-gather.4
  403.3 36.2 all-reduce.3
where the time goes:
time: 449 us
  waiting for transfers between devices  341 us (76%)
  local copies, waits for them, and re-layouts  40.2 us (9%)
  matrix products  36.8 us (8%)
  other arithmetic  17.1 us (4%)
  between operations  14 us (3%)
    all_gather x1, waiting for transfers between devices, on_device(): piece = lax.all_gather(teacher_weight, 'dp', axis=0, tiled=True)  202 us
    unnamed x5, waiting for transfers between devices  85.8 us
    psum x1, waiting for transfers between devices, on_device(): return lax.psum(local_grad.astype(jnp.bfloat16), 'dp').astype(jnp.float32)  36.5 us
    unnamed x26, local copies, waits for them, and re-layouts  17.6 us
    dot_general x1, matrix products, on_device(): jnp.dot(normed_keys, piece[:, 1, :], preferred_element_type=jnp.float32)  16.2 us
    all_gather x1, waiting for transfers between devices, on_device(): piece = lax.all_gather(folded, 'dp', axis=1, tiled=True)  16 us
    dot_general x1, matrix products, on_device(): jnp.dot(normed_query, piece[:, 0, :], preferred_element_type=jnp.float32)  10.2 us
    reshape x1, local copies, waits for them, and re-layouts, on_device(): normed_keys = teacher_normed.reshape(images * tokens, width_t)  9.77 us
  transfers between devices with their start and end apart: 4, of which 4 were waited for; matrix products, arithmetic and copies ran while one was open for 6% of the time, Pallas kernels for 0%

commit v1 on v0

--- a/solution.py
+++ b/solution.py
@@ -8,6 +8,12 @@
 HD_S = 64
 QROWS = 128
 DIVISOR = 72
+
+
+def laid_out(pieces, dim):
+    dims = list(pieces.shape[1:])
+    dims[dim] *= pieces.shape[0]
+    return jnp.moveaxis(pieces, 0, dim).reshape(dims)
 
 
 def layer_norm(values, gain, shift):
@@ -38,7 +44,19 @@
     teacher_normed = layer_norm(teacher_input, teacher_gain, 0.0).astype(jnp.bfloat16)
     normed_query = teacher_normed[:, :QROWS].reshape(images * QROWS, width_t)
     normed_keys = teacher_normed.reshape(images * tokens, width_t)
-    piece = lax.all_gather(teacher_weight, "dp", axis=0, tiled=True)
+    count = lax.axis_size("dp")
+    pairs = [(i, (i + 1) % count) for i in range(count)]
+    back = [(b, a) for a, b in pairs]
+    lower, upper = ([], [])
+    for step in range(count - 1):
+        if step % 2 == 0:
+            lower.append(lax.ppermute(lower[-1] if lower else teacher_weight, "dp", pairs))
+        else:
+            upper.append(lax.ppermute(upper[-1] if upper else teacher_weight, "dp", back))
+    tiles = jnp.stack([*lower[::-1], teacher_weight, *upper])
+    offset = lax.axis_index("dp") - len(lower)
+    tiles = tiles[(jnp.arange(count) - offset) % count]
+    piece = laid_out(tiles, 0)
     new_query = jnp.dot(normed_query, piece[:, 0, :], preferred_element_type=jnp.float32)
     new_keys = jnp.dot(normed_keys, piece[:, 1, :], preferred_element_type=jnp.float32)
     teacher_query = (

time: 449 us -> 980 us (2.18)
  other arithmetic: 17.1 us -> 296 us
  local copies, waits for them, and re-layouts: 40.2 us -> 201 us
  waiting for transfers between devices: 341 us -> 421 us
    ppermute x0 -> x3, waiting for transfers between devices: none -> 279 us  [the longest x2 279 us: on_device(): lax.ppermute(lower[-1] if lower else teacher_weight, 'dp', pairs)]
    unnamed x0 -> x1, other arithmetic: none -> 205 us
    all_gather x1 -> x0, waiting for transfers between devices: 202 us -> none  [on_device(): piece = lax.all_gather(teacher_weight, 'dp', axis=0, tiled=True)]
    gather x0 -> x33, local copies, waits for them, and re-layouts: none -> 124 us
    another operation x0 -> x1, other arithmetic: none -> 73.5 us  [on_device(): tiles = jnp.stack([*lower[::-1], teacher_weight, *upper])]
    unnamed x26 -> x30, local copies, waits for them, and re-layouts: 17.6 us -> 57.2 us
    unnamed x5 -> x4, waiting for transfers between devices: 85.8 us -> 89.6 us
  transfers between devices with their start and end apart: 4 -> 6, of which waited for: 4 -> 5; matrix products, arithmetic and copies ran while one was open for 6% -> 3% of each run, Pallas kernels for 0% -> 0%
where the time goes in v1:
time: 980 us; the launch traced here: 974 us
  waiting for transfers between devices  421 us (43%)
  other arithmetic  296 us (30%)
  local copies, waits for them, and re-layouts  201 us (21%)
  matrix products  36.6 us (4%)
  between operations  14.3 us (1%)
    ppermute x2, waiting for transfers between devices, on_device(): lax.ppermute(lower[-1] if lower else teacher_weight, 'dp', pairs)  279 us
    unnamed x1, other arithmetic  205 us
    gather x32, local copies, waits for them, and re-layouts  93.3 us
    unnamed x4, waiting for transfers between devices  89.6 us
    another operation x1, other arithmetic, on_device(): tiles = jnp.stack([*lower[::-1], teacher_weight, *upper])  73.5 us
    unnamed x30, local copies, waits for them, and re-layouts  57.2 us
    psum x1, waiting for transfers between devices, on_device(): return lax.psum(local_grad.astype(jnp.bfloat16), 'dp').astype(jnp.float32)  36.5 us
    gather x1, local copies, waits for them, and re-layouts, on_device(): tiles = tiles[(jnp.arange(count) - offset) % count]  30.2 us
  transfers between devices with their start and end apart: 6, of which 5 were waited for; matrix products, arithmetic and copies ran while one was open for 3% of the time, Pallas kernels for 0%

profile of v1, /device:TPU:0, one launch (start us, length us, event | category | flops | bytes accessed | tf_op | source)
XLA Modules:
  0.0 973.6 jit_solution(4974045684985609441)
XLA Ops:
  7.0 1.9 collective-permute-start.2
  8.9 201.2 %collective-permute-done = bf16[1536,2,1536]{2,1,0:T(2,128)(2,1)} collective-permute-done((bf16[1536,2,1536]{2,1,0:T(2,128)(2,1)}, bf16[1536,2,1536]{2,1,0:T(2,128)(2,1)}, u32[]{:S(2)}, u32[]{:S(2)}) %collective-permute-start) | collective-permute-done | bytes 9437216 | tf_op jit(solution)/shard_map/ppermute | solution.py:53
  210.1 2.5 collective-permute-start.1
  212.7 6.3 convert_reduce_fusion
  219.0 3.5 fusion.5
  222.5 4.4 fusion.7
  226.9 2.7 copy-done.1
  229.6 7.0 reshape.134
  236.7 77.9 %collective-permute-done.1 = bf16[1536,2,1536]{2,1,0:T(2,128)(2,1)} collective-permute-done((bf16[1536,2,1536]{2,1,0:T(2,128)(2,1)}, bf16[1536,2,1536]{2,1,0:T(2,128)(2,1)}, u32[]{:S(2)}, u32[]{:S(2)}) %collective-permute-start.1) | collective-permute-done | bytes 9437216 | tf_op jit(solution)/shard_map/ppermute | solution.py:53
  314.6 73.5 %pad_maximum_fusion = bf16[4,1536,2,1536]{3,2,1,0:T(2,128)(2,1)} fusion(bf16[1,1536,2,1536]{3,2,1,0:T(2,128)(2,1)} %bitcast.13, bf16[1,1536,2,1536]{3,2,1,0:T(2,128)(2,1)} %bitcast.119, bf16[1,1536,2,1536]{3,2,1,0:T(2,128)(2,1)} %bitcast.11, bf16[1,1536,2,1536]{3,2,1,0:T(2,128)(2,1)} %bitcast.10), kind=kLoop, calls=%fused_computation.9 | loop fusion | flops 56623104 | bytes 75497472 | tf_op jit(solution)/shard_map/stack | solution.py:56
  388.1 30.2 %fusion.61 = (bf16[4,384,2,1536]{3,2,1,0:T(2,128)(2,1)}, bf16[4,384,2,1536]{3,2,1,0:T(2,128)(2,1)}, bf16[4,384,2,1536]{3,2,1,0:T(2,128)(2,1)}, bf16[4,384,2,1536]{3,2,1,0:T(2,128)(2,1)}) fusion(bf16[4,1536,2,1536]{3,2,1,0:T(2,128)(2,1)} %pad_maximum_fusion), kind=kLoop, calls=%fused_computation.92 | loop fusion | bytes 75497472 | tf_op jit(solution)/shard_map/gather | solution.py:58
  418.3 6.1 broadcast.122.clone.3
  424.4 23.4 %while.4 = (s32[]{:T(128)}, bf16[4,384,2,1536]{3,2,1,0:T(2,128)(2,1)}, s32[4,1]{0,1:T(1,128)S(1)}, bf16[4,384,2,1536]{3,2,1,0:T(2,128)(2,1)}, s32[]{:T(128)}) while((s32[]{:T(128)}, bf16[4,384,2,1536]{3,2,1,0:T(2,128)(2,1)}, s32[4,1]{0,1:T(1,128)S(1)}, bf16[4,384,2,1536]{3,2,1,0:T(2,128)(2,1)}, s32[]{:T(128)}) %tuple.64), condition=%wide.while_cond, body=%wide.while_body.sunk | while | flops 2 | bytes 4719689 | solution.py:58
  425.0 5.3 dynamic-slice_dynamic-update-slice_fusion.8
  430.9 5.3 dynamic-slice_dynamic-update-slice_fusion.8
  436.7 5.3 dynamic-slice_dynamic-update-slice_fusion.8
  442.6 5.2 dynamic-slice_dynamic-update-slice_fusion.8
  447.8 6.1 broadcast.122.clone.2
  454.0 23.3 %while.5 = (s32[]{:T(128)}, bf16[4,384,2,1536]{3,2,1,0:T(2,128)(2,1)}, s32[4,1]{0,1:T(1,128)S(1)}, bf16[4,384,2,1536]{3,2,1,0:T(2,128)(2,1)}, s32[]{:T(128)}) while((s32[]{:T(128)}, bf16[4,384,2,1536]{3,2,1,0:T(2,128)(2,1)}, s32[4,1]{0,1:T(1,128)S(1)}, bf16[4,384,2,1536]{3,2,1,0:T(2,128)(2,1)}, s32[]{:T(128)}) %tuple.73), condition=%wide.while_cond.1, body=%wide.while_body.1.sunk | while | flops 2 | bytes 4719689 | solution.py:58
  454.6 5.2 dynamic-slice_dynamic-update-slice_fusion.9
  460.4 5.3 dynamic-slice_dynamic-update-slice_fusion.9
  466.2 5.3 dynamic-slice_dynamic-update-slice_fusion.9
  472.1 5.2 dynamic-slice_dynamic-update-slice_fusion.9
  477.3 6.1 broadcast.122.clone.1
  483.4 23.4 %while.6 = (s32[]{:T(128)}, bf16[4,384,2,1536]{3,2,1,0:T(2,128)(2,1)}, s32[4,1]{0,1:T(1,128)S(1)}, bf16[4,384,2,1536]{3,2,1,0:T(2,128)(2,1)}, s32[]{:T(128)}) while((s32[]{:T(128)}, bf16[4,384,2,1536]{3,2,1,0:T(2,128)(2,1)}, s32[4,1]{0,1:T(1,128)S(1)}, bf16[4,384,2,1536]{3,2,1,0:T(2,128)(2,1)}, s32[]{:T(128)}) %tuple.74), condition=%wide.while_cond.2, body=%wide.while_body.2.sunk | while | flops 2 | bytes 4719689 | solution.py:58
  484.0 5.3 dynamic-slice_dynamic-update-slice_fusion.10
  489.8 5.3 dynamic-slice_dynamic-update-slice_fusion.10
  495.7 5.3 dynamic-slice_dynamic-update-slice_fusion.10
  501.5 5.2 dynamic-slice_dynamic-update-slice_fusion.10
  506.8 6.1 broadcast.122.clone
  512.9 23.4 %while.7 = (s32[]{:T(128)}, bf16[4,384,2,1536]{3,2,1,0:T(2,128)(2,1)}, s32[4,1]{0,1:T(1,128)S(1)}, bf16[4,384,2,1536]{3,2,1,0:T(2,128)(2,1)}, s32[]{:T(128)}) while((s32[]{:T(128)}, bf16[4,384,2,1536]{3,2,1,0:T(2,128)(2,1)}, s32[4,1]{0,1:T(1,128)S(1)}, bf16[4,384,2,1536]{3,2,1,0:T(2,128)(2,1)}, s32[]{:T(128)}) %tuple.75), condition=%wide.while_cond.3, body=%wide.while_body.3.sunk | while | flops 2 | bytes 4719689 | solution.py:58
  513.7 5.2 dynamic-slice_dynamic-update-slice_fusion.11
  519.4 5.2 dynamic-slice_dynamic-update-slice_fusion.11
  525.3 5.3 dynamic-slice_dynamic-update-slice_fusion.11
  531.1 5.2 dynamic-slice_dynamic-update-slice_fusion.11
  536.3 204.7 %pad_maximum_fusion.1 = bf16[4,1536,2,1536]{3,2,1,0:T(2,128)(2,1)} fusion(bf16[4,384,2,1536]{3,2,1,0:T(2,128)(2,1)} %get-tuple-element.36, bf16[4,384,2,1536]{3,2,1,0:T(2,128)(2,1)} %get-tuple-element.28, bf16[4,384,2,1536]{3,2,1,0:T(2,128)(2,1)} %get-tuple-element.20, bf16[4,384,2,1536]{3,2,1,0:T(2,128)(2,1)} %get-tuple-element.12), kind=kLoop, calls=%fused_computation.10 | loop fusion | flops 56623104 | bytes 75497472
  741.0 26.0 %copy.104 = bf16[4,1536,2,1536]{3,1,0,2:T(8,128)(2,1)} copy(bf16[4,1536,2,1536]{3,2,1,0:T(2,128)(2,1)} %pad_maximum_fusion.1) | data formatting | bytes 75497472
  767.0 10.2 %fusion.10 = bf16[256,1536]{1,0:T(8,128)(2,1)} fusion(bf16[256,6144]{1,0:T(8,128)(2,1)S(1)} %bitcast.116, bf16[6144,2,1536]{2,0,1:T(8,128)(2,1)} %bitcast.117), kind=kOutput, calls=%fused_computation.29 | convolution fusion | flops 4832624640 | bytes 22806528 | tf_op jit(solution)/shard_map/dot_general | solution.py:60
  777.2 2.4 reshape.228
  779.6 16.0 %fusion.8 = bf16[514,1536]{1,0:T(8,128)(2,1)S(1)} fusion(bf16[514,6144]{1,0:T(8,128)(2,1)} %reshape.134, bf16[6144,2,1536]{2,0,1:T(8,128)(2,1)} %bitcast.118), kind=kOutput, calls=%fused_computation.25 | convolution fusion | flops 9702214656 | bytes 26843136 | tf_op jit(solution)/shard_map/dot_general | solution.py:61
  795.6 2.4 reshape.135
  798.0 3.1 fusion.63
  802.6 2.9 copy.109
  806.9 89.6 %all-reduce.6.cloned.1.call-done = bf16[16,2,128,257]{2,1,3,0:T(2,128)(2,1)} async-done(((bf16[16,2,128,257]{2,1,3,0:T(2,128)(2,1)}), bf16[16,2,128,257]{2,1,3,0:T(2,128)(2,1)}) %all-reduce.6.cloned.1.call-update) | async-done | bytes 2105360
  904.5 16.2 %all-gather.2.cloned.1.call-done = bf16[4,8,128,257]{2,0,3,1:T(4,128)(2,1)} async-done(((bf16[4,2,128,257]{2,0,3,1:T(4,128)(2,1)}), bf16[4,8,128,257]{2,0,3,1:T(4,128)(2,1)}) %all-gather.2.cloned.1.call-update) | async-done | bytes 2105360 | tf_op jit(solution)/shard_map/all_gather | solution.py:84
  920.7 2.4 fusion.17
  927.8 36.5 %all-reduce.4.cloned.1.call-done = bf16[1024,512]{0,1:T(8,128)(2,1)} async-done(((bf16[1024,512]{0,1:T(8,128)(2,1)}), bf16[1024,512]{0,1:T(8,128)(2,1)}) %all-reduce.4.cloned.1.call-update) | async-done | bytes 1048592 | tf_op jit(solution)/shard_map/psum | solution.py:137
  964.3 2.6 copy.118
  (75 shorter events, 24.4 us)
Async XLA Ops:
  6.5 889.9 %all-reduce.6.cloned.1.call-start = ((), (), s32[]{:S(2)}) async-start(), calls=%async_computation.2 | async-start | bytes 4210688
  6.5 203.6 %collective-permute-start = (bf16[1536,2,1536]{2,1,0:T(2,128)(2,1)}, bf16[1536,2,1536]{2,1,0:T(2,128)(2,1)}, u32[]{:S(2)}, u32[]{:S(2)}) collective-permute-start(bf16[1536,2,1536]{2,1,0:T(2,128)(2,1)} %param.11), channel_id=1, source_target_pairs={{0,1},{1,2},{2,3},{3,0},{4,5},{5,6},{6,7},{7,4},{8,9},{9,10},{10,1... | collective-permute-start | bytes 28311560 | tf_op jit(solution)/shard_map/ppermute | solution.py:53
  7.0 229.6 %collective-permute-start.2 = (bf16[1536,2,1536]{2,1,0:T(2,128)(2,1)}, bf16[1536,2,1536]{2,1,0:T(2,128)(2,1)}, u32[]{:S(2)}, u32[]{:S(2)}) collective-permute-start(bf16[1536,2,1536]{2,1,0:T(2,128)(2,1)} %param.11), channel_id=1, source_target_pairs={{1,0},{2,1},{3,2},{0,3},{5,4},{6,5},{7,6},{4,7},{9,8},{10,9},{11,1... | collective-permute-start | bytes 28311560 | tf_op jit(solution)/shard_map/ppermute | solution.py:55
  210.1 104.4 %collective-permute-start.1 = (bf16[1536,2,1536]{2,1,0:T(2,128)(2,1)}, bf16[1536,2,1536]{2,1,0:T(2,128)(2,1)}, u32[]{:S(2)}, u32[]{:S(2)}) collective-permute-start(bf16[1536,2,1536]{2,1,0:T(2,128)(2,1)} %collective-permute-done), channel_id=1, source_target_pairs={{0,1},{1,2},{2,3},{3,0},{4,5},{5,6},{6,7},{7,4},{8,9},{9,10},{10,1... | collective-permute-start | bytes 28311560 | tf_op jit(solution)/shard_map/ppermute | solution.py:53
  212.7 6.3 copy-start
  219.0 3.5 copy-start.5
  226.9 2.7 copy-start.1
  741.0 26.0 %slice-start = ((bf16[2,257,6144]{2,1,0:T(8,128)(2,1)}), bf16[2,128,6144]{2,1,0:T(8,128)(2,1)S(1)}, s32[]{:S(2)}) async-start(bf16[2,257,6144]{2,1,0:T(8,128)(2,1)} %copy-done.1), calls=%async_computation.3 | async-start | bytes 6291456 | tf_op jit(solution)/shard_map/slice | solution.py:45
  801.2 0.7 copy-start.6
  802.6 3.0 copy-start.10
  805.6 93.4 %copy-start.4 = (bf16[1024,512]{1,0:T(8,128)(2,1)S(1)}, bf16[1024,512]{1,0:T(8,128)(2,1)}, u32[]{:S(2)}) copy-start(bf16[1024,512]{1,0:T(8,128)(2,1)} %param.17) | copy-start | bytes 3145732
  805.6 94.0 %copy-start.2 = (bf16[2,257,1024]{2,0,1:T(2,128)(2,1)S(1)}, bf16[2,257,1024]{2,0,1:T(2,128)(2,1)}, u32[]{:S(2)}) copy-start(bf16[2,257,1024]{2,0,1:T(2,128)(2,1)} %param.14) | copy-start | bytes 3158020
  805.6 115.1 %all-gather.2.cloned.1.call-start = ((), (), s32[]{:S(2)}) async-start(), calls=%async_computation | async-start | bytes 2631680 | tf_op jit(solution)/shard_map/all_gather | solution.py:84
  898.9 1.5 copy-start.7
  898.9 1.5 copy-start.8
  898.9 65.4 %all-reduce.4.cloned.1.call-start = ((), (), s32[]{:S(2)}) async-start(), calls=%async_computation.1 | async-start | bytes 2097152 | tf_op jit(solution)/shard_map/psum | solution.py:137
  900.9 1.0 copy-start.3
  902.4 18.3 %copy-start.9 = (s32[2]{0:T(128)S(1)}, s32[2]{0:T(128)}, u32[]{:S(2)}) copy-start(s32[2]{0:T(128)} %param.13) | copy-start | bytes 28
Sparse Core Ops, SparseCore 0:
  805.7 90.7 all-reduce.5
  899.0 21.6 all-gather.1
  928.0 36.2 all-reduce.3
